TPU v7x, 128 devices: a whole 4x4x4 slice. The times are simulated.
128 devices in a mesh: ctx: 16 (over z, x_lo, core), tp: 8 (over y, x_hi).
Axes of the slice: x: 4 (x_hi: 2, x_lo: 2; x = x_hi * 2 + x_lo), y: 4, z: 4, core: 2. Of those that a mesh axis runs over, the one named last changes fastest.
Arguments:
- projected: bfloat16 [3, 4096, 8192], P(None, 'ctx', 'tp'), may hold values from -6 to 6
- short_taps: float32 [3, 7, 8192], P(None, None, 'tp'), may hold values from -2.4 to 2.4
- range_filter: bfloat16 [64, 1024], P('tp'), may hold values from -0.1875 to 0.1875
- skip_gain: float32 [8192], P('tp'), may hold values from -4 to 4
- out_weight: bfloat16 [8192, 8192], P('ctx', 'tp'), may hold values from -0.0625 to 0.0625
Outputs:
- mixed: bfloat16 [4096, 8192], P('ctx', 'tp')
All inputs are finite; a program needn't handle non-finite values.
Results may differ from a plain program's by a relative error of at most 0.0057.
Values may be sent and summed in bfloat16 or wider, within the bound.
A program may use at most 192 MiB of HBM per device.

v0:
```python
import jax
import jax.numpy as jnp
from jax import lax
from jax.sharding import PartitionSpec as P


def passed_along(block, axis, distance):
    devices = range(lax.axis_size(axis))
    route = [((i - distance) % len(devices), i) for i in devices]
    return lax.ppermute(block, axis, route)


def short_conv(extended, tap_rows, length):
    accumulated = jnp.zeros((length, extended.shape[1]), jnp.float32)
    rim_width = tap_rows.shape[0] - 1
    for lag_index in range(tap_rows.shape[0]):
        window = extended[rim_width - lag_index : rim_width - lag_index + length]
        accumulated = accumulated + tap_rows[lag_index][None, :] * window.astype(jnp.float32)
    return accumulated


def toeplitz_strip(range_filter, length):
    groups, kept = range_filter.shape
    period = kept + 2 * length
    flipped = range_filter[:, ::-1]
    row = jnp.pad(flipped, ((0, 0), (length, period - length - kept)))
    tiled = jnp.tile(row, (1, length + 1))
    start = length - 1
    shifted = tiled[:, start : start + length * (period - 1)].reshape(groups, length, period - 1)
    return shifted[:, :, : kept + length]


def local(projected, short_taps, range_filter, skip_gain, out_weight):
    length = projected.shape[1]
    width_dev = projected.shape[2]
    groups = range_filter.shape[0]
    group_width = width_dev // groups
    rim_width = short_taps.shape[1] - 1
    span_blocks = range_filter.shape[1] // length
    rim_block = passed_along(projected[:, length - rim_width :, :], "ctx", 1)
    extended = jnp.concatenate([rim_block, projected], axis=1)
    query_feat = short_conv(extended[0], short_taps[0], length)
    key_feat = short_conv(extended[1], short_taps[1], length)
    value_feat = short_conv(extended[2], short_taps[2], length)
    mixed_in = (key_feat * value_feat).astype(jnp.bfloat16)
    strip = toeplitz_strip(range_filter, length)
    pieces = [passed_along(mixed_in, "ctx", offset) for offset in range(span_blocks, 0, -1)]
    window = jnp.concatenate(pieces + [mixed_in], axis=0).reshape(-1, groups, group_width)
    toeplitz = jnp.einsum("gam,mgc->agc", strip, window, preferred_element_type=jnp.float32)
    toeplitz = toeplitz.reshape(length, width_dev)
    restored = lax.optimization_barrier(mixed_in).astype(jnp.float32)
    gated_out = (query_feat * (toeplitz + skip_gain[None, :] * restored)).astype(jnp.bfloat16)
    gathered = lax.all_gather(gated_out, "tp", axis=1, tiled=True)
    summed = jnp.dot(
        gathered,
        lax.all_gather(out_weight, "ctx", axis=0, tiled=True),
        preferred_element_type=jnp.float32,
    )
    return summed.astype(jnp.bfloat16)


def solution(mesh):
    placed = (P(None, "ctx", "tp"), P(None, None, "tp"), P("tp", None), P("tp"), P("ctx", "tp"))
    return jax.shard_map(
        local, mesh=mesh, in_specs=placed, out_specs=P("ctx", "tp"), check_vma=False
    )
```

profile of v0, /device:TPU:1, one launch (start us, length us, event | category | flops | bytes accessed | tf_op | source)
XLA Modules:
  0.0 258.7 jit_solution(12750595578099567330)
XLA Ops:
  6.5 0.0 copy-start.1
  6.5 0.0 all-gather.3.cloned.1.call-start
  6.5 0.8 slice.231
  7.4 2.7 %collective-permute-start = (bf16[3,6,1024]{2,1,0:T(8,128)(2,1)S(1)}, bf16[3,6,1024]{2,1,0:T(8,128)(2,1)S(1)}, u32[]{:S(2)}, u32[]{:S(2)}) collective-permute-start(bf16[3,6,1024]{2,1,0:T(8,128)(2,1)S(1)} %slice.231), channel_id=1, source_target_pairs={{120,0},{0,8},{8,16},{16,24},{24,32},{32,40},{40,48},{48,56},{56,6... | collective-permute-start | bytes 110600 | tf_op jit(solution)/shard_map/ppermute | solution.py:10
  10.0 1.4 fusion.59
  11.5 0.8 fusion.60
  12.3 0.0 collective-permute-done
  12.3 5.2 %fusion.4 = bf16[256,1024]{1,0:T(8,128)(2,1)S(1)} fusion(bf16[3,6,1024]{2,1,0:T(8,128)(2,1)S(1)} %collective-permute-done, bf16[3,256,1024]{2,1,0:T(8,128)(2,1)} %param.5, f32[1024]{0:T(1024)S(1)} %bitcast.144, f32[1024]{0:T(1024)S(1)} %bitcast.143, f32[1024]{0:T(1024)S(1)} %bitcast.131, f32[1024]{0:T(1024)S(1)} %bitcast.132, f32[1024]{0:T(1024)S(1)} %bitcast.133, ...), kind=kLoop, calls=%fused_computation.23 | loop fusion | flops 23592960 | bytes 3239936 | tf_op jit(solution)/shard_map/convert_element_type | solution.py:45
  17.5 1.7 collective-permute-start.1
  19.2 2.8 %collective-permute-start.2 = (bf16[256,1024]{1,0:T(8,128)(2,1)S(1)}, bf16[256,1024]{1,0:T(8,128)(2,1)S(1)}, u32[]{:S(2)}, u32[]{:S(2)}) collective-permute-start(bf16[256,1024]{1,0:T(8,128)(2,1)S(1)} %fusion.4), channel_id=1, source_target_pairs={{104,0},{112,8},{120,16},{0,24},{8,32},{16,40},{24,48},{32,56},{40... | collective-permute-start | bytes 1572872 | tf_op jit(solution)/shard_map/ppermute | solution.py:10
  22.0 0.3 collective-permute-start.3
  22.3 1.6 collective-permute-start.4
  23.9 0.0 copy-done.1
  23.9 0.6 rev.3
  24.6 0.4 tile.4
  25.0 3.9 %slice.307 = bf16[8,392960]{1,0:T(8,128)(2,1)} slice(bf16[8,394752]{1,0:T(8,128)(2,1)S(1)} %bitcast.128), slice={[0:8], [255:393215]} | slice | bytes 12574720 | tf_op jit(solution)/shard_map/slice | solution.py:29
  28.9 14.7 %reshape.143 = bf16[3143680]{0:T(1024)(128)(2,1)} reshape(bf16[8,392960]{1,0:T(8,128)(2,1)} %slice.307) | data formatting | bytes 12574720
  43.6 13.7 %reshape.120 = bf16[8,256,1535]{2,1,0:T(8,128)(2,1)} reshape(bf16[3143680]{0:T(1024)(128)(2,1)} %reshape.143) | data formatting | bytes 12574720 | tf_op jit(solution)/shard_map/reshape | solution.py:29
  57.4 0.0 collective-permute-done.1
  57.4 0.8 constant_dynamic-update-slice_fusion.4
  58.2 0.9 collective-permute-done.2
  59.1 0.8 constant_dynamic-update-slice_fusion.3
  59.9 0.0 collective-permute-done.3
  59.9 0.8 constant_dynamic-update-slice_fusion.2
  60.7 0.0 collective-permute-done.4
  60.7 0.9 constant_dynamic-update-slice_fusion.1
  61.6 0.9 constant_dynamic-update-slice_fusion
  62.5 3.0 %copy.8 = bf16[1280,1024]{0,1:T(8,128)(2,1)S(1)} copy(bf16[1280,1024]{1,0:T(8,128)(2,1)} %constant_dynamic-update-slice_fusion) | data formatting | bytes 5242880 | tf_op jit(solution)/shard_map/concatenate | solution.py:48
  65.4 0.0 copy-start.2
  65.5 5.3 %fusion = f32[8,128,256]{2,1,0:T(8,128)} fusion(bf16[1280,8,128]{0,2,1:T(8,128)(2,1)S(1)} %bitcast.129, bf16[8,256,1535]{2,1,0:T(8,128)(2,1)} %reshape.120), kind=kOutput, calls=%fused_computation.17 | convolution fusion | flops 671088640 | bytes 8912896 | tf_op jit(solution)/shard_map/gam,mgc->agc/dot_general | solution.py:49
  70.8 0.0 copy-start
  70.8 1.7 copy.9
  72.4 0.0 copy-done.2
  72.4 0.0 copy-done
  72.5 1.8 fusion.18
  74.3 0.0 all-gather.3.cloned.1.call-update
  74.3 0.0 all-gather.5.cloned.1.call-start
  74.4 0.7 all-gather.5.cloned.1.call-update
  75.1 72.0 %all-gather.3.cloned.1.call-done = bf16[256,8192]{1,0:T(8,128)(2,1)} async-done(((bf16[256,1024]{1,0:T(8,128)(2,1)}), bf16[256,8192]{1,0:T(8,128)(2,1)}) %all-gather.3.cloned.1.call-update) | async-done | bytes 4194320 | tf_op jit(solution)/shard_map/all_gather | solution.py:53
  147.1 92.4 %all-gather.5.cloned.1.call-done = bf16[8192,1024]{1,0:T(8,128)(2,1)} async-done(((bf16[512,1024]{1,0:T(8,128)(2,1)}), bf16[8192,1024]{1,0:T(8,128)(2,1)}) %all-gather.5.cloned.1.call-update) | async-done | bytes 16777232 | tf_op jit(solution)/shard_map/all_gather | solution.py:56
  239.5 12.3 %convolution_convert_fusion = bf16[256,1024]{1,0:T(8,128)(2,1)} fusion(bf16[256,8192]{1,0:T(8,128)(2,1)} %all-gather.3.cloned.1.call-done, bf16[8192,1024]{1,0:T(8,128)(2,1)} %all-gather.5.cloned.1.call-done), kind=kOutput, calls=%fused_computation.19 | convolution fusion | flops 4295229440 | bytes 21495808 | tf_op jit(solution)/shard_map/dot_general | solution.py:54
  (1 shorter events, 0.0 us)
Async XLA Ops:
  6.5 17.4 %copy-start.1 = (bf16[8,1024]{1,0:T(8,128)(2,1)S(1)}, bf16[8,1024]{1,0:T(8,128)(2,1)}, u32[]{:S(2)}) copy-start(bf16[8,1024]{1,0:T(8,128)(2,1)} %param.7) | copy-start | bytes 49156
  6.5 140.6 %all-gather.3.cloned.1.call-start = ((), (), s32[]{:S(2)}) async-start(), calls=%async_computation | async-start | bytes 4718592 | tf_op jit(solution)/shard_map/all_gather | solution.py:53
  7.4 4.9 %collective-permute-start = (bf16[3,6,1024]{2,1,0:T(8,128)(2,1)S(1)}, bf16[3,6,1024]{2,1,0:T(8,128)(2,1)S(1)}, u32[]{:S(2)}, u32[]{:S(2)}) collective-permute-start(bf16[3,6,1024]{2,1,0:T(8,128)(2,1)S(1)} %slice.231), channel_id=1, source_target_pairs={{120,0},{0,8},{8,16},{16,24},{24,32},{32,40},{40,48},{48,56},{56,6... | collective-permute-start | bytes 110600 | tf_op jit(solution)/shard_map/ppermute | solution.py:10
  17.5 39.8 %collective-permute-start.1 = (bf16[256,1024]{1,0:T(8,128)(2,1)S(1)}, bf16[256,1024]{1,0:T(8,128)(2,1)S(1)}, u32[]{:S(2)}, u32[]{:S(2)}) collective-permute-start(bf16[256,1024]{1,0:T(8,128)(2,1)S(1)} %fusion.4), channel_id=1, source_target_pairs={{96,0},{104,8},{112,16},{120,24},{0,32},{8,40},{16,48},{24,56},{32... | collective-permute-start | bytes 1572872 | tf_op jit(solution)/shard_map/ppermute | solution.py:10
  19.2 39.8 %collective-permute-start.2 = (bf16[256,1024]{1,0:T(8,128)(2,1)S(1)}, bf16[256,1024]{1,0:T(8,128)(2,1)S(1)}, u32[]{:S(2)}, u32[]{:S(2)}) collective-permute-start(bf16[256,1024]{1,0:T(8,128)(2,1)S(1)} %fusion.4), channel_id=1, source_target_pairs={{104,0},{112,8},{120,16},{0,24},{8,32},{16,40},{24,48},{32,56},{40... | collective-permute-start | bytes 1572872 | tf_op jit(solution)/shard_map/ppermute | solution.py:10
  22.0 37.8 %collective-permute-start.3 = (bf16[256,1024]{1,0:T(8,128)(2,1)S(1)}, bf16[256,1024]{1,0:T(8,128)(2,1)S(1)}, u32[]{:S(2)}, u32[]{:S(2)}) collective-permute-start(bf16[256,1024]{1,0:T(8,128)(2,1)S(1)} %fusion.4), channel_id=1, source_target_pairs={{112,0},{120,8},{0,16},{8,24},{16,32},{24,40},{32,48},{40,56},{48,... | collective-permute-start | bytes 1572872 | tf_op jit(solution)/shard_map/ppermute | solution.py:10
  22.3 38.4 %collective-permute-start.4 = (bf16[256,1024]{1,0:T(8,128)(2,1)S(1)}, bf16[256,1024]{1,0:T(8,128)(2,1)S(1)}, u32[]{:S(2)}, u32[]{:S(2)}) collective-permute-start(bf16[256,1024]{1,0:T(8,128)(2,1)S(1)} %fusion.4), channel_id=1, source_target_pairs={{120,0},{0,8},{8,16},{16,24},{24,32},{32,40},{40,48},{48,56},{56,6... | collective-permute-start | bytes 1572872 | tf_op jit(solution)/shard_map/ppermute | solution.py:10
  65.4 7.0 %copy-start.2 = (f32[1024]{0:T(1024)S(1)}, f32[1024]{0:T(1024)}, u32[]{:S(2)}) copy-start(f32[1024]{0:T(1024)} %param.8) | copy-start | bytes 12292
  70.8 1.7 copy-start
  74.3 165.1 %all-gather.5.cloned.1.call-start = ((), (), s32[]{:S(2)}) async-start(), calls=%async_computation.1 | async-start | bytes 17825792 | tf_op jit(solution)/shard_map/all_gather | solution.py:56
Sparse Core Ops, SparseCore 0:
  74.5 72.6 all-gather.2
  148.8 90.6 all-gather.4
where the time goes:
time: 259 us
  waiting for transfers between devices  166 us (64%)
  local copies, waits for them, and re-layouts  45.5 us (18%)
  matrix products  17.6 us (7%)
  between operations  13.5 us (5%)
  starting transfers between devices  9.11 us (4%)
  other arithmetic  7.04 us (3%)
    all_gather x1, waiting for transfers between devices, local(): lax.all_gather(out_weight, 'ctx', axis=0, tiled=True)  92.4 us
    all_gather x1, waiting for transfers between devices, local(): gathered = lax.all_gather(gated_out, 'tp', axis=1, tiled=True)  72 us
    unnamed x11, local copies, waits for them, and re-layouts  18.2 us
    reshape x1, local copies, waits for them, and re-layouts, toeplitz_strip(): tiled[:, start:start + length * (period - 1)]  13.7 us
    dot_general x1, matrix products, local(): jnp.dot(gathered, lax.all_gather(out_weight, 'ctx', axis=0, tiled=True),...  12.3 us
    ppermute x5, starting transfers between devices, passed_along(): return lax.ppermute(block, axis, route)  9.06 us
    dot_general x1, matrix products, local(): jnp.einsum('gam,mgc->agc', strip, window, preferred_element_type=jnp.floa...  5.29 us
    convert_element_type x1, other arithmetic, local(): mixed_in = (key_feat * value_feat).astype(jnp.bfloat16)  5.2 us
  transfers between devices with their start and end apart: 7, of which 3 were waited for; matrix products, arithmetic and copies ran while one was open for 15% of the time, Pallas kernels for 0%

commit v1 on v0

--- a/solution.py
+++ b/solution.py
@@ -1,7 +1,23 @@
+import functools
 import jax
 import jax.numpy as jnp
 from jax import lax
 from jax.sharding import PartitionSpec as P
+
+
+def choose_the_columns(local_array, chip_axis):
+    return jnp.concatenate(
+        lax.all_to_all(
+            jnp.stack(lax.axis_size(chip_axis) * [local_array]),
+            chip_axis,
+            split_axis=0,
+            concat_axis=0,
+        ),
+        axis=1,
+    )
+
+
+fit_stacks_all_all = functools.partial(choose_the_columns, chip_axis="tp")
 
 
 def passed_along(block, axis, distance):
@@ -50,7 +66,7 @@
     toeplitz = toeplitz.reshape(length, width_dev)
     restored = lax.optimization_barrier(mixed_in).astype(jnp.float32)
     gated_out = (query_feat * (toeplitz + skip_gain[None, :] * restored)).astype(jnp.bfloat16)
-    gathered = lax.all_gather(gated_out, "tp", axis=1, tiled=True)
+    gathered = fit_stacks_all_all(gated_out)
     summed = jnp.dot(
         gathered,
         lax.all_gather(out_weight, "ctx", axis=0, tiled=True),

time: 259 us -> 201 us (0.78)
  the two profiles are of different devices: /device:TPU:1 before, /device:TPU:96 now
where the time goes in v1:
time: 201 us; the launch traced here: 200 us
  blocking collectives  81.7 us (41%)
  local copies, waits for them, and re-layouts  48.5 us (24%)
  waiting for transfers between devices  29.1 us (14%)
  matrix products  18.6 us (9%)
  between operations  13.5 us (7%)
  other arithmetic  6.96 us (3%)
    all_to_all x1, blocking collectives, choose_the_columns(): lax.all_to_all(jnp.stack(lax.axis_size(chip_axis) * [local_array]), chip_...  81.7 us
    ppermute x5, waiting for transfers between devices, passed_along(): return lax.ppermute(block, axis, route)  28.4 us
    unnamed x11, local copies, waits for them, and re-layouts  18.2 us
    reshape x1, local copies, waits for them, and re-layouts, toeplitz_strip(): tiled[:, start:start + length * (period - 1)]  13.7 us
    dot_general x1, matrix products, local(): jnp.dot(gathered, lax.all_gather(out_weight, 'ctx', axis=0, tiled=True),...  12.4 us
    dot_general x1, matrix products, local(): jnp.einsum('gam,mgc->agc', strip, window, preferred_element_type=jnp.floa...  6.23 us
    concatenate x2, local copies, waits for them, and re-layouts, local(): jnp.concatenate(pieces + [mixed_in], axis=0)  5.29 us
    convert_element_type x1, other arithmetic, local(): mixed_in = (key_feat * value_feat).astype(jnp.bfloat16)  5.11 us
  transfers between devices with their start and end apart: 6, of which 3 were waited for; matrix products, arithmetic and copies ran while one was open for 31% of the time, Pallas kernels for 0%

profile of v1, /device:TPU:96, one launch (start us, length us, event | category | flops | bytes accessed | tf_op | source)
XLA Modules:
  0.0 200.0 jit_solution(17628808848456681576)
XLA Ops:
  6.5 0.0 copy-start.1
  6.5 0.0 all-gather.2.cloned.1.call-start
  6.5 0.7 all-gather.2.cloned.1.call-update
  7.3 0.8 slice.231
  8.1 0.1 collective-permute-start
  8.2 1.4 fusion.59
  9.6 0.8 fusion.60
  10.4 2.1 %collective-permute-done = bf16[3,6,1024]{2,1,0:T(8,128)(2,1)S(1)} collective-permute-done((bf16[3,6,1024]{2,1,0:T(8,128)(2,1)S(1)}, bf16[3,6,1024]{2,1,0:T(8,128)(2,1)S(1)}, u32[]{:S(2)}, u32[]{:S(2)}) %collective-permute-start) | collective-permute-done | bytes 36896 | tf_op jit(solution)/shard_map/ppermute | solution.py:26
  12.6 5.1 %fusion.4 = bf16[256,1024]{1,0:T(8,128)(2,1)S(1)} fusion(bf16[3,6,1024]{2,1,0:T(8,128)(2,1)S(1)} %collective-permute-done, bf16[3,256,1024]{2,1,0:T(8,128)(2,1)} %param.5, f32[1024]{0:T(1024)S(1)} %bitcast.148, f32[1024]{0:T(1024)S(1)} %bitcast.147, f32[1024]{0:T(1024)S(1)} %bitcast.135, f32[1024]{0:T(1024)S(1)} %bitcast.136, f32[1024]{0:T(1024)S(1)} %bitcast.137, ...), kind=kLoop, calls=%fused_computation.23 | loop fusion | flops 23592960 | bytes 3239936 | tf_op jit(solution)/shard_map/convert_element_type | solution.py:61
  17.7 1.0 collective-permute-start.1
  18.7 0.0 collective-permute-start.2
  18.7 0.4 collective-permute-start.3
  19.2 0.1 collective-permute-start.4
  19.3 0.0 copy-done.1
  19.3 0.6 rev.3
  19.9 0.4 tile.4
  20.3 3.9 %slice.307 = bf16[8,392960]{1,0:T(8,128)(2,1)} slice(bf16[8,394752]{1,0:T(8,128)(2,1)S(1)} %bitcast.131), slice={[0:8], [255:393215]} | slice | bytes 12574720 | tf_op jit(solution)/shard_map/slice | solution.py:45
  24.2 14.7 %reshape.153 = bf16[3143680]{0:T(1024)(128)(2,1)} reshape(bf16[8,392960]{1,0:T(8,128)(2,1)} %slice.307) | data formatting | bytes 12574720
  39.0 13.7 %reshape.128 = bf16[8,256,1535]{2,1,0:T(8,128)(2,1)} reshape(bf16[3143680]{0:T(1024)(128)(2,1)} %reshape.153) | data formatting | bytes 12574720 | tf_op jit(solution)/shard_map/reshape | solution.py:45
  52.7 13.2 %collective-permute-done.1 = bf16[256,1024]{1,0:T(8,128)(2,1)S(1)} collective-permute-done((bf16[256,1024]{1,0:T(8,128)(2,1)S(1)}, bf16[256,1024]{1,0:T(8,128)(2,1)S(1)}, u32[]{:S(2)}, u32[]{:S(2)}) %collective-permute-start.1) | collective-permute-done | bytes 524320 | tf_op jit(solution)/shard_map/ppermute | solution.py:26
  65.9 0.9 constant_dynamic-update-slice_fusion.4
  66.8 13.1 %collective-permute-done.2 = bf16[256,1024]{1,0:T(8,128)(2,1)S(1)} collective-permute-done((bf16[256,1024]{1,0:T(8,128)(2,1)S(1)}, bf16[256,1024]{1,0:T(8,128)(2,1)S(1)}, u32[]{:S(2)}, u32[]{:S(2)}) %collective-permute-start.2) | collective-permute-done | bytes 524320 | tf_op jit(solution)/shard_map/ppermute | solution.py:26
  79.9 0.8 constant_dynamic-update-slice_fusion.3
  80.7 0.0 collective-permute-done.3
  80.7 0.8 constant_dynamic-update-slice_fusion.2
  81.5 0.0 collective-permute-done.4
  81.5 0.8 constant_dynamic-update-slice_fusion.1
  82.4 0.8 constant_dynamic-update-slice_fusion
  83.2 4.5 %copy.8 = bf16[1280,1024]{0,1:T(8,128)(2,1)} copy(bf16[1280,1024]{1,0:T(8,128)(2,1)} %constant_dynamic-update-slice_fusion) | data formatting | bytes 5242880 | tf_op jit(solution)/shard_map/concatenate | solution.py:64
  87.7 0.0 copy-start.2
  87.7 6.2 %fusion = f32[8,128,256]{2,1,0:T(8,128)} fusion(bf16[1280,8,128]{0,2,1:T(8,128)(2,1)} %bitcast.133, bf16[8,256,1535]{2,1,0:T(8,128)(2,1)} %reshape.128), kind=kOutput, calls=%fused_computation.17 | convolution fusion | flops 671088640 | bytes 8912896 | tf_op jit(solution)/shard_map/gam,mgc->agc/dot_general | solution.py:65
  93.9 0.0 copy-start
  93.9 1.7 copy.9
  95.6 0.0 copy-done.2
  95.6 0.1 copy-done
  95.7 1.8 fusion.18
  97.5 1.2 copy.10
  98.8 0.3 stack.2
  99.1 81.7 %all_to_all.5 = bf16[8,256,1024]{1,2,0:T(8,128)(2,1)} all-to-all(bf16[8,256,1024]{1,2,0:T(8,128)(2,1)S(1)} %stack.2), channel_id=1, replica_groups=mesh['ctx'=16,'tp'=8] {'tp'}, dimensions={0} | all-to-all | bytes 8388608 | tf_op jit(solution)/shard_map/all_to_all | solution.py:10
  180.8 0.0 all-gather.2.cloned.1.call-done
  180.8 12.4 %convolution_convert_fusion = bf16[256,1024]{1,0:T(8,128)(2,1)} fusion(bf16[256,8192]{0,1:T(8,128)(2,1)} %bitcast.132, bf16[8192,1024]{1,0:T(8,128)(2,1)} %all-gather.2.cloned.1.call-done), kind=kOutput, calls=%fused_computation.19 | convolution fusion | flops 4295229440 | bytes 21495808 | tf_op jit(solution)/shard_map/dot_general | solution.py:70
  (1 shorter events, 0.0 us)
Async XLA Ops:
  6.5 12.8 %copy-start.1 = (bf16[8,1024]{1,0:T(8,128)(2,1)S(1)}, bf16[8,1024]{1,0:T(8,128)(2,1)}, u32[]{:S(2)}) copy-start(bf16[8,1024]{1,0:T(8,128)(2,1)} %param.7) | copy-start | bytes 49156
  6.5 174.2 %all-gather.2.cloned.1.call-start = ((), (), s32[]{:S(2)}) async-start(), calls=%async_computation.1 | async-start | bytes 17825792 | tf_op jit(solution)/shard_map/all_gather | solution.py:72
  8.1 4.5 %collective-permute-start = (bf16[3,6,1024]{2,1,0:T(8,128)(2,1)S(1)}, bf16[3,6,1024]{2,1,0:T(8,128)(2,1)S(1)}, u32[]{:S(2)}, u32[]{:S(2)}) collective-permute-start(bf16[3,6,1024]{2,1,0:T(8,128)(2,1)S(1)} %slice.231), channel_id=1, source_target_pairs={{120,0},{0,8},{8,16},{16,24},{24,32},{32,40},{40,48},{48,56},{56,6... | collective-permute-start | bytes 110600 | tf_op jit(solution)/shard_map/ppermute | solution.py:26
  17.7 48.2 %collective-permute-start.1 = (bf16[256,1024]{1,0:T(8,128)(2,1)S(1)}, bf16[256,1024]{1,0:T(8,128)(2,1)S(1)}, u32[]{:S(2)}, u32[]{:S(2)}) collective-permute-start(bf16[256,1024]{1,0:T(8,128)(2,1)S(1)} %fusion.4), channel_id=1, source_target_pairs={{96,0},{104,8},{112,16},{120,24},{0,32},{8,40},{16,48},{24,56},{32... | collective-permute-start | bytes 1572872 | tf_op jit(solution)/shard_map/ppermute | solution.py:26
  18.7 61.1 %collective-permute-start.2 = (bf16[256,1024]{1,0:T(8,128)(2,1)S(1)}, bf16[256,1024]{1,0:T(8,128)(2,1)S(1)}, u32[]{:S(2)}, u32[]{:S(2)}) collective-permute-start(bf16[256,1024]{1,0:T(8,128)(2,1)S(1)} %fusion.4), channel_id=1, source_target_pairs={{104,0},{112,8},{120,16},{0,24},{8,32},{16,40},{24,48},{32,56},{40... | collective-permute-start | bytes 1572872 | tf_op jit(solution)/shard_map/ppermute | solution.py:26
  18.7 62.0 %collective-permute-start.3 = (bf16[256,1024]{1,0:T(8,128)(2,1)S(1)}, bf16[256,1024]{1,0:T(8,128)(2,1)S(1)}, u32[]{:S(2)}, u32[]{:S(2)}) collective-permute-start(bf16[256,1024]{1,0:T(8,128)(2,1)S(1)} %fusion.4), channel_id=1, source_target_pairs={{112,0},{120,8},{0,16},{8,24},{16,32},{24,40},{32,48},{40,56},{48,... | collective-permute-start | bytes 1572872 | tf_op jit(solution)/shard_map/ppermute | solution.py:26
  19.2 62.4 %collective-permute-start.4 = (bf16[256,1024]{1,0:T(8,128)(2,1)S(1)}, bf16[256,1024]{1,0:T(8,128)(2,1)S(1)}, u32[]{:S(2)}, u32[]{:S(2)}) collective-permute-start(bf16[256,1024]{1,0:T(8,128)(2,1)S(1)} %fusion.4), channel_id=1, source_target_pairs={{120,0},{0,8},{8,16},{16,24},{24,32},{32,40},{40,48},{48,56},{56,6... | collective-permute-start | bytes 1572872 | tf_op jit(solution)/shard_map/ppermute | solution.py:26
  87.7 7.9 %copy-start.2 = (f32[1024]{0:T(1024)S(1)}, f32[1024]{0:T(1024)}, u32[]{:S(2)}) copy-start(f32[1024]{0:T(1024)} %param.8) | copy-start | bytes 12292
  93.9 1.8 copy-start
Sparse Core Ops, SparseCore 0:
  9.0 157.2 all-gather.1
